TPU v7x, 32 devices: a whole 2x2x4 slice. The times are simulated.
32 devices in a mesh: blk: 4 (over y, x), team: 4 (over z), dp: 2 (over core).
Axes of the slice: x: 2, y: 2, z: 4, core: 2. Of those that a mesh axis runs over, the one named last changes fastest.
Arguments:
- hidden: bfloat16 [1024, 28672], P(('blk', 'dp'), 'team'), may hold values from -6 to 6
- out_grad: bfloat16 [1024, 8192], P(('blk', 'dp'), 'team'), may hold values from -0.1875 to 0.1875
- act_rows: int32 [4, 64, 12], P('team'), may hold values from 0 to 55, as said below
- col_owner: int32 [64], replicated, may hold values from 0 to 3, as said below
Outputs:
- gradients: float32 [4, 4, 288, 128, 128], P('team', 'blk', 'dp')
- scores: float32 [4, 4, 288], P('team', 'blk', 'dp')
Inputs may be any that keep to these rules, and one draw needn't show every extreme that they name: For each t and c the 12 entries act_rows[t, c, :] are distinct. `col_owner`: some owner holds exactly 24 block columns and no owner holds more.
All inputs are finite; a program needn't handle non-finite values.
Results may differ from a plain program's by a relative error of at most 0.0003.
Values may be sent and summed in bfloat16 or wider, within the bound.
A program may use at most 192 MiB of HBM per device.

v0:
```python
import functools

import jax
import jax.numpy as jnp
from jax import lax
from jax.experimental import pallas as pl
from jax.experimental.pallas import tpu as pltpu
from jax.sharding import PartitionSpec as P

BS = 128
MESH = pl.DeviceIdType.MESH
CHUNKS = 4
HALVES = 2


epsilon = 1e-06


def owner_tables(col_owner, owners_count, capacity):
    column_blocks = col_owner.shape[0]
    owners = jnp.arange(owners_count, dtype=jnp.int32)
    onehot = (col_owner[:, None] == owners[None, :]).astype(jnp.int32)
    column_rank = jnp.sum((jnp.cumsum(onehot, axis=0) - onehot) * onehot, axis=1)
    slot_ids = jnp.arange(capacity, dtype=jnp.int32)
    matches = (col_owner[None, None, :] == owners[:, None, None]) & (
        column_rank[None, None, :] == slot_ids[None, :, None]
    )
    owned_all = jnp.sum(
        matches.astype(jnp.int32) * jnp.arange(column_blocks, dtype=jnp.int32)[None, None, :],
        axis=2,
    )
    return owned_all, jnp.any(matches, axis=2)


def gather_kernel(
    cols_ref, hid_ref, grad_ref, hfull, gfull, gz, gcol, snd, send_sem, recv_sem, local_sem
):
    teams = lax.axis_size("team")
    b, t, d = lax.axis_index("blk"), lax.axis_index("team"), lax.axis_index("dp")
    y, x = b // 2, b % 2
    panels, panel_rows, _ = hfull.shape
    part_rows = panel_rows // teams
    part_cols = grad_ref.shape[1]
    picks = cols_ref.shape[1]
    chunk = panel_rows // CHUNKS

    def plane(sy, sx, sd):
        oy = 1 - y if sy else y
        ox = 1 - x if sx else x
        return oy * 2 + ox, (1 - d if sd else d)

    def panel_of(sy, sx, sd):
        ob, od = plane(sy, sx, sd)
        return ob * 2 + od

    def device(sy, sx, sd):
        ob, od = plane(sy, sx, sd)
        return (ob, t, od)

    mine = panel_of(0, 0, 0)
    flips = [(sy, sx, sd) for sy in (0, 1) for sx in (0, 1) for sd in (0, 1)][1:]

    barrier = pltpu.get_barrier_semaphore()
    for flip in flips:
        pl.semaphore_signal(barrier, inc=1, device_id=device(*flip), device_id_type=MESH)
    for s in range(1, teams):
        pl.semaphore_signal(
            barrier, inc=1, device_id=(b, (t + s) % teams, d), device_id_type=MESH
        )
    pl.semaphore_wait(barrier, len(flips) + teams - 1)

    counter = [0]

    def remote(src, dst, target, slot=None):
        if slot is None:
            slot = counter[0]
            counter[0] += 1
        return pltpu.make_async_remote_copy(
            src_ref=src,
            dst_ref=dst,
            send_sem=send_sem.at[slot],
            recv_sem=recv_sem.at[slot],
            device_id=target,
            device_id_type=MESH,
        )

    sent = []

    def rows_of(c):
        return pl.ds(c * chunk, chunk)

    def send_own(flip, c):
        copy = remote(hid_ref.at[rows_of(c)], hfull.at[mine, rows_of(c)], device(*flip))
        copy.start()
        sent.append(copy)
        return copy

    def forward(panel, flip, c):
        piece = hfull.at[panel, rows_of(c)]
        copy = remote(piece, piece, device(*flip))
        copy.start()
        sent.append(copy)
        return copy

    half_rows = part_rows // HALVES

    def part(k, half):
        return pl.ds(k * part_rows + half * half_rows, half_rows)

    def held(half):
        return pl.ds(half * half_rows, half_rows)

    def quarter(k):
        return pl.ds(k * part_cols, part_cols)

    own_grad, stage1 = [], []
    for half in range(HALVES):
        for s in range(1, teams):
            target = (t + s) % teams
            copy = remote(
                grad_ref.at[part(target, half)],
                gz.at[held(half), quarter(t)],
                (b, target, d),
            )
            copy.start()
            stage1.append(copy)
            sent.append(copy)
        own_grad.append(
            pltpu.make_async_copy(
                grad_ref.at[part(t, half)],
                gz.at[held(half), quarter(t)],
                local_sem.at[1 + half],
            )
        )
        own_grad[half].start()

    order_x = list(range(CHUNKS))
    order_y = order_x[CHUNKS // 2 :] + order_x[: CHUNKS // 2]
    X, Y, SIB = (0, 1, 0), (1, 0, 0), (0, 0, 1)
    from_x, from_y, from_sib = {}, {}, []
    from_x[order_x[0]] = send_own(X, order_x[0])
    from_y[order_y[0]] = send_own(Y, order_y[0])
    own_hidden = pltpu.make_async_copy(hid_ref, hfull.at[mine], local_sem.at[0])
    own_hidden.start()

    own_pick, stage2 = [], []
    for half in range(HALVES):
        own_grad[half].wait()
        for copy in stage1[half * (teams - 1) : (half + 1) * (teams - 1)]:
            copy.wait_recv()
        rows = slice(half * half_rows, (half + 1) * half_rows)
        for c in range(gcol.shape[1]):
            gcol[half, c] = gz[rows, c * BS : (c + 1) * BS]

        def pick(p, carry):
            for j in range(picks):
                snd[half, p, :, j * BS : (j + 1) * BS] = gcol[half, cols_ref[p, j]]
            return carry

        lax.fori_loop(0, panels, pick, 0)
        landing = gfull.at[mine, part(t, half)]
        for flip in flips:
            copy = remote(snd.at[half, panel_of(*flip)], landing, device(*flip))
            copy.start()
            stage2.append(copy)
            sent.append(copy)
        own_pick.append(
            pltpu.make_async_copy(
                snd.at[half, mine], landing, local_sem.at[1 + HALVES + half]
            )
        )
        own_pick[half].start()

    for i in range(1, CHUNKS):
        from_x[order_x[i]] = send_own(X, order_x[i])
        from_y[order_y[i]] = send_own(Y, order_y[i])
    for c in range(CHUNKS):
        from_sib.append(send_own(SIB, c))

    chain_base = counter[0]
    counter[0] += 2 * (teams - 1) * HALVES

    def chain(up, k, shard, target, half):
        piece = gfull.at[:, part(shard, half)]
        step = k if up else teams - 1 + k
        return remote(piece, piece, (b, target, d), chain_base + step * HALVES + half)

    def chain_send(k, half, wait):
        @pl.when((t < teams - 1) & (t - k >= 0))
        def _():
            copy = chain(True, k, t - k, t + 1, half)
            copy.wait_send() if wait else copy.start()

        @pl.when((t > 0) & (t + k < teams))
        def _():
            copy = chain(False, k, t + k, t - 1, half)
            copy.wait_send() if wait else copy.start()

    def chain_recv(k, half):
        @pl.when(t - 1 - k >= 0)
        def _():
            chain(True, k, t - 1 - k, t - 1, half).wait_recv()

        @pl.when(t + 1 + k < teams)
        def _():
            chain(False, k, t + 1 + k, t + 1, half).wait_recv()

    def chain_step(k):
        for half in range(HALVES):
            chain_recv(k, half)
            if k < teams - 2:
                chain_send(k + 1, half, False)

    for half in range(HALVES):
        own_pick[half].wait()
        for copy in stage2[half * len(flips) : (half + 1) * len(flips)]:
            copy.wait_recv()
        chain_send(0, half, False)

    panel_x, panel_y, panel_xy = panel_of(*X), panel_of(*Y), panel_of(1, 1, 0)
    from_xy = {}
    steps = 0
    for i in range(CHUNKS):
        cx, cy = order_x[i], order_y[i]
        from_x[cx].wait_recv()
        if i < CHUNKS // 2:
            from_xy[cx] = forward(panel_x, Y, cx)
        from_sib.append(forward(panel_x, SIB, cx))
        from_y[cy].wait_recv()
        if i < CHUNKS // 2:
            from_xy[cy] = forward(panel_y, X, cy)
        from_sib.append(forward(panel_y, SIB, cy))
        if i % 2 == 1 and steps < teams - 1:
            chain_step(steps)
            steps += 1
    for c in order_x:
        c = order_x[c // 2] if c % 2 == 0 else order_y[c // 2]
        from_xy[c].wait_recv()
        from_sib.append(forward(panel_xy, SIB, c))
    while steps < teams - 1:
        chain_step(steps)
        steps += 1
    for copy in from_sib:
        copy.wait_recv()
    for copy in sent:
        copy.wait_send()
    for k in range(teams - 1):
        for half in range(HALVES):
            chain_send(k, half, True)
    own_hidden.wait()


def gather(columns, hidden, out_grad, panels):
    teams = lax.axis_size("team")
    panel_rows, units = hidden.shape
    picks = columns.shape[1]
    copies = (3 * (teams - 1) + panels - 1) * HALVES + 7 * CHUNKS
    half_rows = panel_rows // teams // HALVES
    hbm = pl.BlockSpec(memory_space=pl.ANY)
    return pl.pallas_call(
        gather_kernel,
        out_shape=(
            jax.ShapeDtypeStruct((panels, panel_rows, units), hidden.dtype),
            jax.ShapeDtypeStruct((panels, panel_rows, picks * BS), out_grad.dtype),
        ),
        in_specs=[pl.BlockSpec(memory_space=pltpu.SMEM), hbm, hbm],
        out_specs=(hbm, hbm),
        scratch_shapes=[
            pltpu.VMEM((panel_rows // teams, teams * out_grad.shape[1]), out_grad.dtype),
            pltpu.VMEM(
                (HALVES, teams * out_grad.shape[1] // BS, half_rows, BS), out_grad.dtype
            ),
            pltpu.VMEM((HALVES, panels, half_rows, picks * BS), out_grad.dtype),
            pltpu.SemaphoreType.DMA((copies,)),
            pltpu.SemaphoreType.DMA((copies,)),
            pltpu.SemaphoreType.DMA((1 + 2 * HALVES,)),
        ],
        compiler_params=pltpu.CompilerParams(collective_id=0, has_side_effects=True),
    )(columns, hidden, out_grad)


def block_kernel(rows_ref, alive_ref, h_ref, g_ref, out_ref, ssq_ref):
    j = pl.program_id(0)
    per_column = out_ref.shape[0]
    scale = alive_ref[j].astype(jnp.float32)
    g = g_ref[...]
    for k in range(0, per_column, 4):
        group = []
        for i in range(k, k + 4):
            r = rows_ref[j * per_column + i]
            group.append(h_ref[:, pl.ds(pl.multiple_of(r * BS, BS), BS)])
        product = lax.dot_general(
            jnp.concatenate(group, axis=1),
            g,
            (((0,), (0,)), ((), ())),
            preferred_element_type=jnp.float32,
        )
        block = product.reshape(4, BS, BS) * scale
        out_ref[k : k + 4] = block
        ssq_ref[0, k : k + 4, :] = jnp.sum(block * block, axis=1)


def blocks(rows, alive, hidden, grad):
    picks = alive.shape[0]
    per_column = rows.shape[0] // picks
    tokens, units = hidden.shape
    return pl.pallas_call(
        block_kernel,
        out_shape=(
            jax.ShapeDtypeStruct((picks * per_column, BS, BS), jnp.float32),
            jax.ShapeDtypeStruct((picks, per_column, BS), jnp.float32),
        ),
        grid_spec=pltpu.PrefetchScalarGridSpec(
            num_scalar_prefetch=2,
            grid=(picks,),
            in_specs=[
                pl.BlockSpec(
                    (tokens, units), lambda j, *_: (0, 0), pipeline_mode=pl.Buffered(1)
                ),
                pl.BlockSpec((tokens, BS), lambda j, *_: (0, j)),
            ],
            out_specs=(
                pl.BlockSpec((per_column, BS, BS), lambda j, *_: (j, 0, 0)),
                pl.BlockSpec((1, per_column, BS), lambda j, *_: (j, 0, 0)),
            ),
        ),
        compiler_params=pltpu.CompilerParams(dimension_semantics=("arbitrary",)),
    )(rows, alive, hidden, grad)


def in_plane(hidden, out_grad, act_rows, col_owner):
    owners_count, cores = lax.axis_size("blk"), lax.axis_size("dp")
    column_blocks = col_owner.shape[0]
    capacity = min(3 * column_blocks // (2 * owners_count), 3 * column_blocks // 4)
    owned_all, alive_all = owner_tables(col_owner, owners_count, capacity)
    panels = owners_count * cores
    picks = capacity // cores
    columns = owned_all.reshape(panels, picks)
    mine = lax.axis_index("blk") * cores + lax.axis_index("dp")
    columns_mine = lax.dynamic_index_in_dim(columns, mine, 0, keepdims=False)
    alive_mine = lax.dynamic_index_in_dim(
        alive_all.reshape(panels, picks), mine, 0, keepdims=False
    ).astype(jnp.int32)
    rows = jnp.take(act_rows[0], columns_mine, axis=0).reshape(-1)
    hidden_all, grad_mine = gather(columns, hidden, out_grad, panels)
    tokens = panels * hidden.shape[0]
    gradients, ssq = blocks(
        rows,
        alive_mine,
        hidden_all.reshape(tokens, hidden.shape[1]),
        grad_mine.reshape(tokens, picks * BS),
    )
    mean = jnp.sum(ssq, axis=2).reshape(-1) * (1.0 / (BS * BS))
    scores = jnp.sqrt(mean + epsilon)
    return (gradients[None, None], scores[None, None])


def on_device(hidden, out_grad, act_rows, col_owner):
    owners_count = lax.axis_size("blk")
    owner_index = lax.axis_index("blk")
    column_blocks = col_owner.shape[0]
    capacity = min(3 * column_blocks // (2 * owners_count), 3 * column_blocks // 4)
    per_column = act_rows.shape[2]
    owned_all, alive_all = owner_tables(col_owner, owners_count, capacity)
    owned_mine = lax.dynamic_index_in_dim(owned_all, owner_index, 0, keepdims=False)
    alive_mine = lax.dynamic_index_in_dim(alive_all, owner_index, 0, keepdims=False)
    block_rows = jnp.take(act_rows[0], owned_mine, axis=0).reshape(-1)
    grad_full = lax.all_gather(out_grad, "team", axis=1, tiled=True)
    grad_mask = alive_mine.astype(jnp.bfloat16)[None, :, None]
    hidden_piece = lax.all_gather(hidden, "blk", axis=0, tiled=True)
    grad_piece = lax.all_gather(grad_full, "blk", axis=0, tiled=True)
    count_rows = grad_piece.shape[0]
    picked_grad = (
        jnp.take(grad_piece.reshape(count_rows, column_blocks, BS), owned_mine, axis=1) * grad_mask
    )
    hidden_blocks = hidden_piece.reshape(count_rows, -1, BS)
    picked_hidden = jnp.take(hidden_blocks, block_rows, axis=1).reshape(
        count_rows, capacity, per_column, BS
    )
    partial_value = jnp.einsum(
        "ncki,ncj->ckij", picked_hidden, picked_grad, preferred_element_type=jnp.float32
    )
    partial_value = partial_value.reshape(capacity * per_column, BS, BS)
    gradients = lax.psum_scatter(partial_value, "dp", scatter_dimension=0, tiled=True)
    scores = jnp.sqrt(jnp.mean(gradients * gradients, axis=(1, 2)) + epsilon)
    return (gradients[None, None], scores[None, None])


def solution(mesh):
    in_specs = (P(("blk", "dp"), "team"), P(("blk", "dp"), "team"), P("team", None, None), P())
    out_specs = (P("team", "blk", "dp", None, None), P("team", "blk", "dp"))
    square = mesh.shape["blk"] == 4 and mesh.shape["dp"] == 2
    return jax.shard_map(
        in_plane if square else on_device,
        mesh=mesh,
        in_specs=in_specs,
        out_specs=out_specs,
        check_vma=False,
    )
```

profile of v0, /device:TPU:0, one launch (start us, length us, event | category | flops | bytes accessed | tf_op | source)
XLA Modules:
  0.0 107.3 jit_solution(6852364457405215764)
XLA Ops:
  0.6 0.7 iota_compare_fusion.2
  1.3 0.8 copy.7
  2.1 0.7 fusion.1
  2.8 0.1 reduce_window_sum.11
  2.9 0.8 select_reduce_fusion
  3.8 0.2 and_reduce_fusion
  3.9 0.2 fusion
  4.1 0.1 reshape.127
  4.2 0.5 fusion.2.alive_ref
  4.7 0.1 reshape.126.cols_ref
  4.8 0.0 copy-start
  4.8 0.6 gather_fusion
  5.4 0.1 broadcast_select_fusion
  5.4 0.7 select_n.34.rows_ref
  6.1 0.0 copy-done
  6.1 79.1 %shard_map.59 = (bf16[8,128,7168]{2,1,0:T(8,128)(2,1)}, bf16[8,128,1536]{2,1,0:T(8,128)(2,1)}) custom-call(s32[8,12]{1,0:T(8,128)} %copy-done, bf16[128,7168]{1,0:T(8,128)(2,1)} %hid_ref.1, bf16[128,2048]{1,0:T(8,128)(2,1)} %grad_ref.1), custom_call_target="tpu_custom_call" | custom-call | tf_op jit(solution)/shard_map/pallas_call | solution.py:260
  85.2 20.4 %shard_map.60 = (f32[144,128,128]{2,1,0:T(8,128)}, f32[12,12,128]{2,1,0:T(8,128)}) custom-call(s32[144]{0:T(256)} %select_n.34.rows_ref, s32[12]{0:T(128)} %fusion.2.alive_ref, bf16[1024,7168]{1,0:T(8,128)(2,1)} %bitcast.12, bf16[1024,1536]{1,0:T(8,128)(2,1)} %bitcast.13), custom_call_target="tpu_custom_call" | custom-call | tf_op jit(solution)/shard_map/pallas_call | solution.py:307
  105.6 1.0 reduce_sum.29
  106.6 0.6 sqrt.14
  (5 shorter events, 0.0 us)
Async XLA Ops:
  4.8 1.3 %copy-start = (s32[8,12]{1,0:T(8,128)}, s32[8,12]{1,0:T(8,128)S(1)}, u32[]{:S(2)}) copy-start(s32[8,12]{1,0:T(8,128)S(1)} %reshape.126.cols_ref) | copy-start | bytes 1156
where the time goes:
time: 108 us; the launch traced here: 107 us
  Pallas kernels  99.5 us (92%)
  other arithmetic  4.27 us (4%)
  local copies, waits for them, and re-layouts  2.8 us (3%)
    pallas_call x1, Pallas kernels, gather(): pl.pallas_call(gather_kernel, out_shape=(jax.ShapeDtypeStruct((panels, pa...  79.1 us
    pallas_call x1, Pallas kernels, blocks(): pl.pallas_call(block_kernel, out_shape=(jax.ShapeDtypeStruct((picks * per...  20.4 us

commit v1 on v0

v1 whole, which is shorter than its diff:
```python
import jax
import jax.numpy as jnp
from jax import lax
from jax.experimental import pallas as pl
from jax.experimental.pallas import tpu as pltpu
from jax.sharding import PartitionSpec as P

BS = 128
MESH = pl.DeviceIdType.MESH
HALVES = 2
GROUP = 4


epsilon = 1e-06


def owner_tables(col_owner, owners_count, capacity):
    column_blocks = col_owner.shape[0]
    owners = jnp.arange(owners_count, dtype=jnp.int32)
    onehot = (col_owner[:, None] == owners[None, :]).astype(jnp.int32)
    column_rank = jnp.sum((jnp.cumsum(onehot, axis=0) - onehot) * onehot, axis=1)
    slot_ids = jnp.arange(capacity, dtype=jnp.int32)
    matches = (col_owner[None, None, :] == owners[:, None, None]) & (
        column_rank[None, None, :] == slot_ids[None, :, None]
    )
    owned_all = jnp.sum(
        matches.astype(jnp.int32) * jnp.arange(column_blocks, dtype=jnp.int32)[None, None, :],
        axis=2,
    )
    return owned_all, jnp.any(matches, axis=2)


def shard_of(i, t, teams):
    paired = 2 * jnp.minimum(t, teams - 1 - t)
    step = (i + 1) // 2
    near = t - step if i % 2 else t + step
    far = jnp.where(2 * t < teams, i, teams - 1 - i)
    return jnp.where(i <= paired, near, far)


def columns_of(slot, rows_ref, first, count):
    return [
        slot[:, pl.ds(rows_ref[first + i] * BS, BS)] for i in range(count)
    ]


def products(slot, rows_ref, first, count, g):
    return lax.dot_general(
        jnp.concatenate(columns_of(slot, rows_ref, first, count), axis=1),
        g,
        (((0,), (0,)), ((), ())),
        preferred_element_type=jnp.float32,
    ).reshape(count, BS, BS)


def gather_kernel(cols_ref, rows_ref, hid_ref, grad_ref, last_ref, gfull, acc, *scratch):
    *slots, gz, gcol, snd, send_sem, recv_sem, local_sem = scratch
    slots = [*slots, last_ref]
    teams = lax.axis_size("team")
    b, t, d = lax.axis_index("blk"), lax.axis_index("team"), lax.axis_index("dp")
    y, x = b // 2, b % 2
    panels, picks = cols_ref.shape
    per_column = rows_ref.shape[0] // picks
    part_rows = hid_ref.shape[0] // teams
    half_rows = part_rows // HALVES
    part_cols = grad_ref.shape[1]

    def plane(sy, sx, sd):
        oy = 1 - y if sy else y
        ox = 1 - x if sx else x
        return oy * 2 + ox, (1 - d if sd else d)

    def panel_of(sy, sx, sd):
        ob, od = plane(sy, sx, sd)
        return ob * 2 + od

    def device(sy, sx, sd):
        ob, od = plane(sy, sx, sd)
        return (ob, t, od)

    mine = panel_of(0, 0, 0)
    flips = [(sy, sx, sd) for sy in (0, 1) for sx in (0, 1) for sd in (0, 1)][1:]

    barrier = pltpu.get_barrier_semaphore()
    for flip in flips:
        pl.semaphore_signal(barrier, inc=1, device_id=device(*flip), device_id_type=MESH)
    for s in range(1, teams):
        pl.semaphore_signal(
            barrier, inc=1, device_id=(b, (t + s) % teams, d), device_id_type=MESH
        )
    pl.semaphore_wait(barrier, len(flips) + teams - 1)

    counter = [0, 0]
    sent, local = [], []

    def remote(src, dst, target, slot=None):
        started = slot is None
        if started:
            slot = counter[0]
            counter[0] += 1
        copy = pltpu.make_async_remote_copy(
            src_ref=src,
            dst_ref=dst,
            send_sem=send_sem.at[slot],
            recv_sem=recv_sem.at[slot],
            device_id=target,
            device_id_type=MESH,
        )
        if started:
            copy.start()
            sent.append(copy)
        return copy

    def within(src, dst):
        copy = pltpu.make_async_copy(src, dst, local_sem.at[counter[1]])
        counter[1] += 1
        copy.start()
        return copy

    X, Y, SIB = (0, 1, 0), (1, 0, 0), (0, 0, 1)
    panel_x, panel_y, panel_xy = panel_of(*X), panel_of(*Y), panel_of(1, 1, 0)

    def part(k, half):
        return pl.ds(k * part_rows + half * half_rows, half_rows)

    def place(panel, half):
        return pl.ds((half * panels + panel) * half_rows, half_rows)

    shards = [shard_of(i, t, teams) for i in range(teams)]

    def send_own(flip, i, half):
        return remote(
            hid_ref.at[part(shards[i], half)], slots[i].at[place(mine, half)], device(*flip)
        )

    def forward(panel, flip, i, half):
        piece = slots[i].at[place(panel, half)]
        return remote(piece, piece, device(*flip))

    from_x, from_y, from_xy = {}, {}, {}
    from_sib = [[] for _ in range(teams)]
    own_hidden = [[] for _ in range(teams)]

    def start_own(i):
        from_x[i, 0] = send_own(X, i, 0)
        from_y[i, 1] = send_own(Y, i, 1)
        from_x[i, 1] = send_own(X, i, 1)
        from_y[i, 0] = send_own(Y, i, 0)
        for half in range(HALVES):
            from_sib[i].append(send_own(SIB, i, half))
            own_hidden[i].append(
                within(hid_ref.at[part(shards[i], half)], slots[i].at[place(mine, half)])
            )

    def sibling(panel, i, half):
        from_sib[i].append(forward(panel, SIB, i, half))

    def turn(i):
        from_x[i, 0].wait_recv()
        from_xy[i, 0] = forward(panel_x, Y, i, 0)
        from_y[i, 1].wait_recv()
        from_xy[i, 1] = forward(panel_y, X, i, 1)
        sibling(panel_x, i, 0)
        sibling(panel_y, i, 1)

    def rest(i):
        from_x[i, 1].wait_recv()
        sibling(panel_x, i, 1)
        from_y[i, 0].wait_recv()
        sibling(panel_y, i, 0)

    def corner(i):
        for half in range(HALVES):
            from_xy[i, half].wait_recv()
            sibling(panel_xy, i, half)

    def arrived(i):
        for copy in from_sib[i]:
            copy.wait_recv()
        for copy in own_hidden[i]:
            copy.wait()

    def held(half):
        return pl.ds(half * half_rows, half_rows)

    def quarter(k):
        return pl.ds(k * part_cols, part_cols)

    own_grad, stage1, own_pick, stage2 = [], [], [], []
    for half in range(HALVES):
        for s in range(1, teams):
            target = (t + s) % teams
            stage1.append(
                remote(
                    grad_ref.at[part(target, half)],
                    gz.at[held(half), quarter(t)],
                    (b, target, d),
                )
            )
        own_grad.append(within(grad_ref.at[part(t, half)], gz.at[held(half), quarter(t)]))

    def pick_columns(half):
        own_grad[half].wait()
        for copy in stage1[half * (teams - 1) : (half + 1) * (teams - 1)]:
            copy.wait_recv()
        rows = slice(half * half_rows, (half + 1) * half_rows)
        for c in range(gcol.shape[1]):
            gcol[half, c] = gz[rows, c * BS : (c + 1) * BS]

        def pick(p, carry):
            for j in range(picks):
                snd[half, p, :, j * BS : (j + 1) * BS] = gcol[half, cols_ref[p, j]]
            return carry

        lax.fori_loop(0, panels, pick, 0)
        landing = gfull.at[t, place(mine, half)]
        for flip in flips:
            stage2.append(remote(snd.at[half, panel_of(*flip)], landing, device(*flip)))
        own_pick.append(within(snd.at[half, mine], landing))

    def picked(half):
        own_pick[half].wait()
        for copy in stage2[half * len(flips) : (half + 1) * len(flips)]:
            copy.wait_recv()

    chain_base = send_sem.shape[0] - 2 * (teams - 1) * HALVES
    chain_rows = panels * half_rows

    def chain(up, k, shard, target, half):
        piece = gfull.at[shard, pl.ds(half * chain_rows, chain_rows)]
        step = k if up else teams - 1 + k
        return remote(piece, piece, (b, target, d), chain_base + step * HALVES + half)

    def chain_send(k, half, wait):
        @pl.when((t < teams - 1) & (t - k >= 0))
        def _():
            copy = chain(True, k, t - k, t + 1, half)
            copy.wait_send() if wait else copy.start()

        @pl.when((t > 0) & (t + k < teams))
        def _():
            copy = chain(False, k, t + k, t - 1, half)
            copy.wait_send() if wait else copy.start()

    def chain_step(k, half):
        @pl.when(t - 1 - k >= 0)
        def _():
            chain(True, k, t - 1 - k, t - 1, half).wait_recv()

        @pl.when(t + 1 + k < teams)
        def _():
            chain(False, k, t + 1 + k, t + 1, half).wait_recv()

        if k < teams - 2:
            chain_send(k + 1, half, False)

    def accumulate(i, lo, hi):
        def column(j, carry):
            g = gfull[shards[i], :, pl.ds(pl.multiple_of(j * BS, BS), BS)]
            for k in range(0, per_column, GROUP):
                first = j * per_column + k
                block = products(slots[i], rows_ref, first, GROUP, g)
                at = pl.ds(first, GROUP)
                acc[at] = block if i == 0 else acc[at] + block
            return carry

        lax.fori_loop(lo, hi, column, 0)

    middle = picks // 2
    start_own(0)
    pick_columns(0)
    turn(0)
    pick_columns(1)
    for i in range(teams):
        if i:
            turn(i)
        if i + 1 < teams:
            start_own(i + 1)
        if i == 0:
            picked(0)
            chain_send(0, 0, False)
            rest(0)
            corner(0)
            picked(1)
            chain_send(0, 1, False)
        else:
            chain_step(i - 1, 0)
            accumulate(i - 1, middle, picks)
            rest(i)
            chain_step(i - 1, 1)
            corner(i)
        arrived(i)
        if i + 1 < teams:
            accumulate(i, 0, middle)
    for copy in sent:
        copy.wait_send()
    for k in range(teams - 1):
        for half in range(HALVES):
            chain_send(k, half, True)


def gather(columns, rows, hidden, out_grad):
    teams = lax.axis_size("team")
    panel_rows, units = hidden.shape
    panels, picks = columns.shape
    part_rows = panel_rows // teams
    half_rows = part_rows // HALVES
    group = panels * part_rows
    copies = (3 * (teams - 1) + panels - 1) * HALVES + 7 * HALVES * teams
    locals_ = HALVES * (2 + teams)
    hbm = pl.BlockSpec(memory_space=pl.ANY)
    smem = pl.BlockSpec(memory_space=pltpu.SMEM)
    vmem = pl.BlockSpec(memory_space=pltpu.VMEM)
    return pl.pallas_call(
        gather_kernel,
        out_shape=(
            pltpu.VMEM((group, units), hidden.dtype),
            pltpu.VMEM((teams, group, picks * BS), out_grad.dtype),
            pltpu.VMEM((rows.shape[0], BS, BS), jnp.float32),
        ),
        in_specs=[smem, smem, hbm, hbm],
        out_specs=(vmem, vmem, vmem),
        scratch_shapes=[pltpu.VMEM((group, units), hidden.dtype)] * (teams - 1)
        + [
            pltpu.VMEM((part_rows, teams * out_grad.shape[1]), out_grad.dtype),
            pltpu.VMEM(
                (HALVES, teams * out_grad.shape[1] // BS, half_rows, BS), out_grad.dtype
            ),
            pltpu.VMEM((HALVES, panels, half_rows, picks * BS), out_grad.dtype),
            pltpu.SemaphoreType.DMA((copies,)),
            pltpu.SemaphoreType.DMA((copies,)),
            pltpu.SemaphoreType.DMA((locals_,)),
        ],
        compiler_params=pltpu.CompilerParams(
            collective_id=0, has_side_effects=True, vmem_limit_bytes=24 << 20
        ),
    )(columns, rows, hidden, out_grad)


def finish_kernel(rows_ref, alive_ref, h_ref, g_ref, acc_ref, out_ref, score_ref, ssq):
    j = pl.program_id(0)
    picks = pl.num_programs(0)
    per_column = out_ref.shape[0]
    teams = g_ref.shape[0]
    shard = shard_of(teams - 1, lax.axis_index("team"), teams)
    scale = alive_ref[j].astype(jnp.float32)
    g = g_ref[shard, :, pl.ds(pl.multiple_of(j * BS, BS), BS)]

    @pl.when(j == 0)
    def _():
        ssq[...] = jnp.zeros_like(ssq)

    for k in range(0, per_column, GROUP):
        first = j * per_column + k
        block = acc_ref[pl.ds(first, GROUP)] + products(h_ref, rows_ref, first, GROUP, g)
        block = block * scale
        out_ref[k : k + GROUP] = block
        ssq[pl.ds(first, GROUP), :] = jnp.sum(block * block, axis=1)

    @pl.when(j == picks - 1)
    def _():
        total = jnp.sum(ssq[...].T, axis=0, keepdims=True)
        scores = jnp.sqrt(total * (1.0 / (BS * BS)) + epsilon)
        score_ref[...] = scores[:, : score_ref.shape[1]]


def finish(rows, alive, last, grad, acc):
    picks = alive.shape[0]
    slots = rows.shape[0]
    per_column = slots // picks
    vmem = pl.BlockSpec(memory_space=pltpu.VMEM)
    return pl.pallas_call(
        finish_kernel,
        out_shape=(
            jax.ShapeDtypeStruct((slots, BS, BS), jnp.float32),
            jax.ShapeDtypeStruct((1, slots), jnp.float32),
        ),
        grid_spec=pltpu.PrefetchScalarGridSpec(
            num_scalar_prefetch=2,
            grid=(picks,),
            in_specs=[vmem, vmem, vmem],
            out_specs=(
                pl.BlockSpec((per_column, BS, BS), lambda j, *_: (j, 0, 0)),
                pl.BlockSpec((1, slots), lambda j, *_: (0, 0)),
            ),
            scratch_shapes=[pltpu.VMEM((pl.cdiv(slots, BS) * BS, BS), jnp.float32)],
        ),
        compiler_params=pltpu.CompilerParams(
            dimension_semantics=("arbitrary",), vmem_limit_bytes=12 << 20
        ),
    )(rows, alive, last, grad, acc)


def in_plane(hidden, out_grad, act_rows, col_owner):
    owners_count, cores = lax.axis_size("blk"), lax.axis_size("dp")
    column_blocks = col_owner.shape[0]
    capacity = min(3 * column_blocks // (2 * owners_count), 3 * column_blocks // 4)
    owned_all, alive_all = owner_tables(col_owner, owners_count, capacity)
    panels = owners_count * cores
    picks = capacity // cores
    columns = owned_all.reshape(panels, picks)
    mine = lax.axis_index("blk") * cores + lax.axis_index("dp")
    columns_mine = lax.dynamic_index_in_dim(columns, mine, 0, keepdims=False)
    alive_mine = lax.dynamic_index_in_dim(
        alive_all.reshape(panels, picks), mine, 0, keepdims=False
    ).astype(jnp.int32)
    rows = jnp.take(act_rows[0], columns_mine, axis=0).reshape(-1)
    last, grad, acc = gather(columns, rows, hidden, out_grad)
    gradients, scores = finish(rows, alive_mine, last, grad, acc)
    return (gradients[None, None], scores[None])


def on_device(hidden, out_grad, act_rows, col_owner):
    owners_count = lax.axis_size("blk")
    owner_index = lax.axis_index("blk")
    column_blocks = col_owner.shape[0]
    capacity = min(3 * column_blocks // (2 * owners_count), 3 * column_blocks // 4)
    per_column = act_rows.shape[2]
    owned_all, alive_all = owner_tables(col_owner, owners_count, capacity)
    owned_mine = lax.dynamic_index_in_dim(owned_all, owner_index, 0, keepdims=False)
    alive_mine = lax.dynamic_index_in_dim(alive_all, owner_index, 0, keepdims=False)
    block_rows = jnp.take(act_rows[0], owned_mine, axis=0).reshape(-1)
    grad_full = lax.all_gather(out_grad, "team", axis=1, tiled=True)
    grad_mask = alive_mine.astype(jnp.bfloat16)[None, :, None]
    hidden_piece = lax.all_gather(hidden, "blk", axis=0, tiled=True)
    grad_piece = lax.all_gather(grad_full, "blk", axis=0, tiled=True)
    count_rows = grad_piece.shape[0]
    picked_grad = (
        jnp.take(grad_piece.reshape(count_rows, column_blocks, BS), owned_mine, axis=1) * grad_mask
    )
    hidden_blocks = hidden_piece.reshape(count_rows, -1, BS)
    picked_hidden = jnp.take(hidden_blocks, block_rows, axis=1).reshape(
        count_rows, capacity, per_column, BS
    )
    partial_value = jnp.einsum(
        "ncki,ncj->ckij", picked_hidden, picked_grad, preferred_element_type=jnp.float32
    )
    partial_value = partial_value.reshape(capacity * per_column, BS, BS)
    gradients = lax.psum_scatter(partial_value, "dp", scatter_dimension=0, tiled=True)
    scores = jnp.sqrt(jnp.mean(gradients * gradients, axis=(1, 2)) + epsilon)
    return (gradients[None, None], scores[None, None])


def solution(mesh):
    in_specs = (P(("blk", "dp"), "team"), P(("blk", "dp"), "team"), P("team", None, None), P())
    out_specs = (P("team", "blk", "dp", None, None), P("team", "blk", "dp"))
    square = mesh.shape["blk"] == 4 and mesh.shape["dp"] == 2
    return jax.shard_map(
        in_plane if square else on_device,
        mesh=mesh,
        in_specs=in_specs,
        out_specs=out_specs,
        check_vma=False,
    )
```

time: 108 us -> 96.5 us (0.89)
  Pallas kernels: 99.5 us -> 88.7 us
  other arithmetic: 4.27 us -> 2.75 us
  local copies, waits for them, and re-layouts: 2.8 us -> 4.12 us
    pallas_call x2, Pallas kernels: 99.5 us -> 88.7 us  [the longest x1 79.6 us: gather(): pl.pallas_call(gather_kernel, out_shape=(pltpu.VMEM((group, units), hidde...]
    unnamed x3 -> x5, local copies, waits for them, and re-layouts: 0.78 us -> 3.31 us
where the time goes in v1:
time: 96.5 us; the launch traced here: 96.3 us
  Pallas kernels  88.7 us (92%)
  local copies, waits for them, and re-layouts  4.12 us (4%)
  other arithmetic  2.75 us (3%)
    pallas_call x1, Pallas kernels, gather(): pl.pallas_call(gather_kernel, out_shape=(pltpu.VMEM((group, units), hidde...  79.6 us
    pallas_call x1, Pallas kernels, finish(): pl.pallas_call(finish_kernel, out_shape=(jax.ShapeDtypeStruct((slots, BS,...  9.14 us
    unnamed x5, local copies, waits for them, and re-layouts  3.31 us

profile of v1, /device:TPU:0, one launch (start us, length us, event | category | flops | bytes accessed | tf_op | source)
XLA Modules:
  0.0 96.3 jit_solution(7485237004839198361)
XLA Ops:
  0.6 0.7 iota_compare_fusion.2
  1.3 0.8 copy.7
  2.1 0.7 fusion.1
  2.8 0.1 reduce_window_sum.11
  2.9 0.8 select_reduce_fusion
  3.8 0.2 and_reduce_fusion
  3.9 0.2 fusion
  4.1 0.1 reshape.99
  4.2 0.1 reshape.98.cols_ref
  4.3 0.6 gather_fusion
  4.8 0.1 broadcast_select_fusion
  4.9 0.1 select_n.34.rows_ref
  5.0 0.0 copy-start
  5.0 1.5 %copy-done = bf16[128,7168]{1,0:T(8,128)(2,1)S(1)} copy-done((bf16[128,7168]{1,0:T(8,128)(2,1)S(1)}, bf16[128,7168]{1,0:T(8,128)(2,1)}, u32[]{:S(2)}) %copy-start) | copy-done | bytes 1835032
  6.5 0.0 copy-start.1
  6.5 1.0 %copy-done.1 = bf16[128,2048]{1,0:T(8,128)(2,1)S(1)} copy-done((bf16[128,2048]{1,0:T(8,128)(2,1)S(1)}, bf16[128,2048]{1,0:T(8,128)(2,1)}, u32[]{:S(2)}) %copy-start.1) | copy-done | bytes 524312
  7.5 79.6 %shard_map.59 = (bf16[256,7168]{1,0:T(8,128)(2,1)S(1)}, bf16[4,256,1536]{2,1,0:T(8,128)(2,1)S(1)}, f32[144,128,128]{2,1,0:T(8,128)S(1)}) custom-call(s32[8,12]{1,0:T(8,128)S(1)} %reshape.98.cols_ref, s32[144]{0:T(256)S(1)} %select_n.34.rows_ref, bf16[128,7168]{1,0:T(8,128)(2,1)S(1)} %copy-done, bf16[128,2048]{1,0:T(8,128)(2,1)S(1)} %copy-done.1), custom_call_target="tpu_custom_call" | custom-call | tf_op jit(solution)/shard_map/pallas_call | solution.py:314
  87.1 9.1 %shard_map.60 = (f32[144,128,128]{2,1,0:T(8,128)}, f32[1,144]{1,0:T(1,128)}) custom-call(s32[144]{0:T(256)S(1)} %select_n.34.rows_ref, s32[12]{0:T(128)S(1)} %fusion.2.alive_ref, bf16[256,7168]{1,0:T(8,128)(2,1)S(1)} %get-tuple-element.7.h_ref, bf16[4,256,1536]{2,1,0:T(8,128)(2,1)S(1)} %get-tuple-element.8.g_ref, f32[144,128,128]{2,1,0:T(8,128)S(1)} %get-tuple-element.9.acc_ref), custom_call_target="tpu_custom_call" | custom-call | tf_op jit(solution)/shard_map/pallas_call | solution.py:372
  (5 shorter events, 0.0 us)
Async XLA Ops:
  5.0 1.5 %copy-start = (bf16[128,7168]{1,0:T(8,128)(2,1)S(1)}, bf16[128,7168]{1,0:T(8,128)(2,1)}, u32[]{:S(2)}) copy-start(bf16[128,7168]{1,0:T(8,128)(2,1)} %hid_ref.1) | copy-start | bytes 5505028
  6.5 1.0 %copy-start.1 = (bf16[128,2048]{1,0:T(8,128)(2,1)S(1)}, bf16[128,2048]{1,0:T(8,128)(2,1)}, u32[]{:S(2)}) copy-start(bf16[128,2048]{1,0:T(8,128)(2,1)} %grad_ref.1) | copy-start | bytes 1572868

commit v2 on v1

--- a/solution.py
+++ b/solution.py
@@ -53,14 +53,20 @@
     ).reshape(count, BS, BS)
 
 
-def gather_kernel(cols_ref, rows_ref, hid_ref, grad_ref, last_ref, gfull, acc, *scratch):
-    *slots, gz, gcol, snd, send_sem, recv_sem, local_sem = scratch
+def gather_kernel(
+    owner_ref, act_ref, hid_ref, grad_ref, last_ref, gfull, acc, rows_ref, *scratch
+):
+    *slots, gz, gcol, snd, owner, act, cols_row, cols, send_sem, recv_sem, local_sem = scratch
     slots = [*slots, last_ref]
     teams = lax.axis_size("team")
     b, t, d = lax.axis_index("blk"), lax.axis_index("team"), lax.axis_index("dp")
     y, x = b // 2, b % 2
-    panels, picks = cols_ref.shape
+    _, panels, _, width = snd.shape
+    picks = width // BS
     per_column = rows_ref.shape[0] // picks
+    column_blocks = owner.shape[0]
+    owners_count = lax.axis_size("blk")
+    capacity = panels * picks // owners_count
     part_rows = hid_ref.shape[0] // teams
     half_rows = part_rows // HALVES
     part_cols = grad_ref.shape[1]
@@ -199,17 +205,43 @@
             )
         own_grad.append(within(grad_ref.at[part(t, half)], gz.at[held(half), quarter(t)]))
 
+    def fetch_tables():
+        return [within(owner_ref, owner), within(act_ref, act)]
+
+    def own_columns():
+        lanes = lax.broadcasted_iota(jnp.int32, cols_row.shape, 1)
+        row = jnp.full(cols_row.shape, column_blocks, jnp.int32)
+        ranks = [jnp.int32(k * capacity) for k in range(owners_count)]
+        for c in range(column_blocks):
+            slot = ranks[0]
+            holds = [owner[c] == k for k in range(owners_count)]
+            for k in range(1, owners_count):
+                slot = jnp.where(holds[k], ranks[k], slot)
+            row = jnp.where(lanes == slot, c, row)
+            ranks = [jnp.where(holds[k], ranks[k] + 1, ranks[k]) for k in range(owners_count)]
+        cols_row[...] = row
+
+    def own_rows():
+        def column(j, carry):
+            c = jnp.minimum(cols[0, mine * picks + j], column_blocks - 1)
+            for k in range(per_column):
+                rows_ref[j * per_column + k] = act[k, 0, c]
+            return carry
+
+        lax.fori_loop(0, picks, column, 0)
+
     def pick_columns(half):
         own_grad[half].wait()
         for copy in stage1[half * (teams - 1) : (half + 1) * (teams - 1)]:
             copy.wait_recv()
         rows = slice(half * half_rows, (half + 1) * half_rows)
-        for c in range(gcol.shape[1]):
+        for c in range(column_blocks):
             gcol[half, c] = gz[rows, c * BS : (c + 1) * BS]
+        gcol[half, column_blocks] = jnp.zeros(gcol.shape[2:], gcol.dtype)
 
         def pick(p, carry):
             for j in range(picks):
-                snd[half, p, :, j * BS : (j + 1) * BS] = gcol[half, cols_ref[p, j]]
+                snd[half, p, :, j * BS : (j + 1) * BS] = gcol[half, cols[0, p * picks + j]]
             return carry
 
         lax.fori_loop(0, panels, pick, 0)
@@ -267,7 +299,13 @@
         lax.fori_loop(lo, hi, column, 0)
 
     middle = picks // 2
+    tables = fetch_tables()
     start_own(0)
+    for copy in tables:
+        copy.wait()
+    own_columns()
+    moved = within(cols_row, cols)
+    moved.wait()
     pick_columns(0)
     turn(0)
     pick_columns(1)
@@ -280,6 +318,7 @@
             picked(0)
             chain_send(0, 0, False)
             rest(0)
+            own_rows()
             corner(0)
             picked(1)
             chain_send(0, 1, False)
@@ -299,16 +338,18 @@
             chain_send(k, half, True)
 
 
-def gather(columns, rows, hidden, out_grad):
+def gather(col_owner, act_rows, hidden, out_grad, panels, picks):
     teams = lax.axis_size("team")
     panel_rows, units = hidden.shape
-    panels, picks = columns.shape
+    per_column = act_rows.shape[0]
     part_rows = panel_rows // teams
     half_rows = part_rows // HALVES
     group = panels * part_rows
+    column_blocks = col_owner.shape[0]
+    lanes = pl.cdiv(panels * picks, BS) * BS
     copies = (3 * (teams - 1) + panels - 1) * HALVES + 7 * HALVES * teams
-    locals_ = HALVES * (2 + teams)
-    hbm = pl.BlockSpec(memory_space=pl.ANY)
+    operands = (col_owner, act_rows, hidden, out_grad)
+    hbm = pl.BlockSpec(memory_space=pltpu.HBM)
     smem = pl.BlockSpec(memory_space=pltpu.SMEM)
     vmem = pl.BlockSpec(memory_space=pltpu.VMEM)
     return pl.pallas_call(
@@ -316,58 +357,62 @@
         out_shape=(
             pltpu.VMEM((group, units), hidden.dtype),
             pltpu.VMEM((teams, group, picks * BS), out_grad.dtype),
-            pltpu.VMEM((rows.shape[0], BS, BS), jnp.float32),
+            pltpu.VMEM((picks * per_column, BS, BS), jnp.float32),
+            pltpu.SMEM((picks * per_column,), jnp.int32),
         ),
-        in_specs=[smem, smem, hbm, hbm],
-        out_specs=(vmem, vmem, vmem),
+        in_specs=[hbm] * 4,
+        out_specs=(vmem, vmem, vmem, smem),
         scratch_shapes=[pltpu.VMEM((group, units), hidden.dtype)] * (teams - 1)
         + [
-            pltpu.VMEM((part_rows, teams * out_grad.shape[1]), out_grad.dtype),
-            pltpu.VMEM(
-                (HALVES, teams * out_grad.shape[1] // BS, half_rows, BS), out_grad.dtype
-            ),
+            pltpu.VMEM((part_rows, column_blocks * BS), out_grad.dtype),
+            pltpu.VMEM((HALVES, column_blocks + 1, half_rows, BS), out_grad.dtype),
             pltpu.VMEM((HALVES, panels, half_rows, picks * BS), out_grad.dtype),
+            pltpu.SMEM(col_owner.shape, jnp.int32),
+            pltpu.SMEM(act_rows.shape, jnp.int32),
+            pltpu.VMEM((1, lanes), jnp.int32),
+            pltpu.SMEM((1, lanes), jnp.int32),
             pltpu.SemaphoreType.DMA((copies,)),
             pltpu.SemaphoreType.DMA((copies,)),
-            pltpu.SemaphoreType.DMA((locals_,)),
+            pltpu.SemaphoreType.DMA((HALVES * (2 + teams) + 3,)),
         ],
         compiler_params=pltpu.CompilerParams(
             collective_id=0, has_side_effects=True, vmem_limit_bytes=24 << 20
         ),
-    )(columns, rows, hidden, out_grad)
-
-
-def finish_kernel(rows_ref, alive_ref, h_ref, g_ref, acc_ref, out_ref, score_ref, ssq):
-    j = pl.program_id(0)
-    picks = pl.num_programs(0)
-    per_column = out_ref.shape[0]
+    )(*(pltpu.with_memory_space_constraint(x, pltpu.HBM) for x in operands))
+
+
+def finish_kernel(rows_ref, h_ref, g_ref, acc_ref, out_ref, score_ref, buf, ssq, row, sem):
     teams = g_ref.shape[0]
+    picks = g_ref.shape[2] // BS
+    slots = buf.shape[0]
+    per_column = slots // picks
     shard = shard_of(teams - 1, lax.axis_index("team"), teams)
-    scale = alive_ref[j].astype(jnp.float32)
-    g = g_ref[shard, :, pl.ds(pl.multiple_of(j * BS, BS), BS)]
-
-    @pl.when(j == 0)
-    def _():
-        ssq[...] = jnp.zeros_like(ssq)
-
-    for k in range(0, per_column, GROUP):
-        first = j * per_column + k
-        block = acc_ref[pl.ds(first, GROUP)] + products(h_ref, rows_ref, first, GROUP, g)
-        block = block * scale
-        out_ref[k : k + GROUP] = block
-        ssq[pl.ds(first, GROUP), :] = jnp.sum(block * block, axis=1)
-
-    @pl.when(j == picks - 1)
-    def _():
-        total = jnp.sum(ssq[...].T, axis=0, keepdims=True)
-        scores = jnp.sqrt(total * (1.0 / (BS * BS)) + epsilon)
-        score_ref[...] = scores[:, : score_ref.shape[1]]
-
-
-def finish(rows, alive, last, grad, acc):
-    picks = alive.shape[0]
+    ssq[slots:] = jnp.zeros((ssq.shape[0] - slots, BS), jnp.float32)
+    copies = []
+    for j in range(picks):
+        g = g_ref[shard, :, j * BS : (j + 1) * BS]
+        for first in range(j * per_column, (j + 1) * per_column, GROUP):
+            at = slice(first, first + GROUP)
+            block = acc_ref[at] + products(h_ref, rows_ref, first, GROUP, g)
+            buf[at] = block
+            ssq[at, :] = jnp.sum(block * block, axis=1)
+        done = pl.ds(j * per_column, per_column)
+        copies.append(pltpu.make_async_copy(buf.at[done], out_ref.at[done], sem.at[j]))
+        copies[j].start()
+    total = jnp.sum(ssq[...].T, axis=0, keepdims=True)
+    scores = jnp.sqrt(total * (1.0 / (BS * BS)) + epsilon)
+    row[...] = scores[:, :slots]
+    copies.append(pltpu.make_async_copy(row, score_ref, sem.at[picks]))
+    copies[picks].start()
+    for copy in copies:
+        copy.wait()
+
+
+def finish(rows, last, grad, acc):
     slots = rows.shape[0]
-    per_column = slots // picks
+    picks = grad.shape[2] // BS
+    hbm = pl.BlockSpec(memory_space=pltpu.HBM)
+    smem = pl.BlockSpec(memory_space=pltpu.SMEM)
     vmem = pl.BlockSpec(memory_space=pltpu.VMEM)
     return pl.pallas_call(
         finish_kernel,
@@ -375,38 +420,31 @@
             jax.ShapeDtypeStruct((slots, BS, BS), jnp.float32),
             jax.ShapeDtypeStruct((1, slots), jnp.float32),
         ),
-        grid_spec=pltpu.PrefetchScalarGridSpec(
-            num_scalar_prefetch=2,
-            grid=(picks,),
-            in_specs=[vmem, vmem, vmem],
-            out_specs=(
-                pl.BlockSpec((per_column, BS, BS), lambda j, *_: (j, 0, 0)),
-                pl.BlockSpec((1, slots), lambda j, *_: (0, 0)),
-            ),
-            scratch_shapes=[pltpu.VMEM((pl.cdiv(slots, BS) * BS, BS), jnp.float32)],
-        ),
-        compiler_params=pltpu.CompilerParams(
-            dimension_semantics=("arbitrary",), vmem_limit_bytes=12 << 20
-        ),
-    )(rows, alive, last, grad, acc)
+        in_specs=[smem, vmem, vmem, vmem],
+        out_specs=(hbm, hbm),
+        scratch_shapes=[
+            pltpu.VMEM((slots, BS, BS), jnp.float32),
+            pltpu.VMEM((pl.cdiv(slots, BS) * BS, BS), jnp.float32),
+            pltpu.VMEM((1, slots), jnp.float32),
+            pltpu.SemaphoreType.DMA((picks + 1,)),
+        ],
+        compiler_params=pltpu.CompilerParams(vmem_limit_bytes=20 << 20),
+    )(rows, last, grad, acc)
 
 
 def in_plane(hidden, out_grad, act_rows, col_owner):
     owners_count, cores = lax.axis_size("blk"), lax.axis_size("dp")
     column_blocks = col_owner.shape[0]
     capacity = min(3 * column_blocks // (2 * owners_count), 3 * column_blocks // 4)
-    owned_all, alive_all = owner_tables(col_owner, owners_count, capacity)
-    panels = owners_count * cores
-    picks = capacity // cores
-    columns = owned_all.reshape(panels, picks)
-    mine = lax.axis_index("blk") * cores + lax.axis_index("dp")
-    columns_mine = lax.dynamic_index_in_dim(columns, mine, 0, keepdims=False)
-    alive_mine = lax.dynamic_index_in_dim(
-        alive_all.reshape(panels, picks), mine, 0, keepdims=False
-    ).astype(jnp.int32)
-    rows = jnp.take(act_rows[0], columns_mine, axis=0).reshape(-1)
-    last, grad, acc = gather(columns, rows, hidden, out_grad)
-    gradients, scores = finish(rows, alive_mine, last, grad, acc)
+    last, grad, acc, rows = gather(
+        col_owner,
+        jnp.transpose(act_rows, (2, 0, 1)),
+        hidden,
+        out_grad,
+        owners_count * cores,
+        capacity // cores,
+    )
+    gradients, scores = finish(rows, last, grad, acc)
     return (gradients[None, None], scores[None])
 
 

time: 96.5 us -> 84.6 us (0.88)
  Pallas kernels: 88.7 us -> 83.8 us
  local copies, waits for them, and re-layouts: 4.12 us -> 0 us
  other arithmetic: 2.75 us -> 0 us
    pallas_call x1, Pallas kernels: 9.14 us -> 4.54 us  [finish(): pl.pallas_call(finish_kernel, out_shape=(jax.ShapeDtypeStruct((slots, BS,...]
    unnamed x5 -> x0, local copies, waits for them, and re-layouts: 3.31 us -> none
    reduce_sum x2 -> x0, other arithmetic: 0.99 us -> none  [the longest x1 0.84 us: owner_tables(): jnp.sum((jnp.cumsum(onehot, axis=0) - onehot) * onehot, axis=1)]
where the time goes in v2:
time: 84.6 us; the launch traced here: 84.4 us
  Pallas kernels  83.8 us (99%)
    pallas_call x1, Pallas kernels, gather(): pl.pallas_call(gather_kernel, out_shape=(pltpu.VMEM((group, units), hidde...  79.2 us
    pallas_call x1, Pallas kernels, finish(): pl.pallas_call(finish_kernel, out_shape=(jax.ShapeDtypeStruct((slots, BS,...  4.54 us

profile of v2, /device:TPU:0, one launch (start us, length us, event | category | flops | bytes accessed | tf_op | source)
XLA Modules:
  0.0 84.4 jit_solution(5826168985054711529)
XLA Ops:
  0.6 79.2 %shard_map.59 = (bf16[256,7168]{1,0:T(8,128)(2,1)S(1)}, bf16[4,256,1536]{2,1,0:T(8,128)(2,1)S(1)}, f32[144,128,128]{2,1,0:T(8,128)S(1)}, s32[144]{0:T(256)S(4)}) custom-call(s32[64]{0:T(128)} %owner_ref.1, s32[12,1,64]{2,1,0:T(1,128)} %bitcast.3, bf16[128,7168]{1,0:T(8,128)(2,1)} %hid_ref.1, bf16[128,2048]{1,0:T(8,128)(2,1)} %grad_ref.1), custom_call_target="tpu_custom_call" | custom-call | tf_op jit(solution)/shard_map/pallas_call | solution.py:355
  79.9 4.5 %shard_map.60 = (f32[144,128,128]{2,1,0:T(8,128)}, f32[1,144]{1,0:T(1,128)}) custom-call(s32[144]{0:T(256)S(4)} %get-tuple-element.8.rows_ref, bf16[256,7168]{1,0:T(8,128)(2,1)S(1)} %get-tuple-element.9.h_ref, bf16[4,256,1536]{2,1,0:T(8,128)(2,1)S(1)} %get-tuple-element.10.g_ref, f32[144,128,128]{2,1,0:T(8,128)S(1)} %get-tuple-element.11.acc_ref), custom_call_target="tpu_custom_call" | custom-call | tf_op jit(solution)/shard_map/pallas_call | solution.py:417

commit v3 on v2

--- a/solution.py
+++ b/solution.py
@@ -8,6 +8,7 @@
 BS = 128
 MESH = pl.DeviceIdType.MESH
 HALVES = 2
+PIECES = 4
 GROUP = 4
 
 
@@ -56,7 +57,7 @@
 def gather_kernel(
     owner_ref, act_ref, hid_ref, grad_ref, last_ref, gfull, acc, rows_ref, *scratch
 ):
-    *slots, gz, gcol, snd, owner, act, cols_row, cols, send_sem, recv_sem, local_sem = scratch
+    *slots, gz, gcol, snd, owner, act, cols_row, cols, ready, send_sem, recv_sem, local_sem = scratch
     slots = [*slots, last_ref]
     teams = lax.axis_size("team")
     b, t, d = lax.axis_index("blk"), lax.axis_index("team"), lax.axis_index("dp")
@@ -88,13 +89,27 @@
     flips = [(sy, sx, sd) for sy in (0, 1) for sx in (0, 1) for sd in (0, 1)][1:]
 
     barrier = pltpu.get_barrier_semaphore()
-    for flip in flips:
-        pl.semaphore_signal(barrier, inc=1, device_id=device(*flip), device_id_type=MESH)
-    for s in range(1, teams):
-        pl.semaphore_signal(
-            barrier, inc=1, device_id=(b, (t + s) % teams, d), device_id_type=MESH
-        )
-    pl.semaphore_wait(barrier, len(flips) + teams - 1)
+    X, Y, SIB = (0, 1, 0), (1, 0, 0), (0, 0, 1)
+    below, above = (t > 0).astype(jnp.int32), (t < teams - 1).astype(jnp.int32)
+
+    def greet(sem):
+        for flip in (X, Y, SIB):
+            pl.semaphore_signal(sem, inc=1, device_id=device(*flip), device_id_type=MESH)
+
+        @pl.when(t > 0)
+        def _():
+            pl.semaphore_signal(sem, inc=1, device_id=(b, t - 1, d), device_id_type=MESH)
+
+        @pl.when(t < teams - 1)
+        def _():
+            pl.semaphore_signal(sem, inc=1, device_id=(b, t + 1, d), device_id_type=MESH)
+
+    def met(sem):
+        pl.semaphore_wait(sem, 3 + below + above)
+
+    greet(barrier)
+    met(barrier)
+    greet(ready.at[0])
 
     counter = [0, 0]
     sent, local = [], []
@@ -123,7 +138,6 @@
         copy.start()
         return copy
 
-    X, Y, SIB = (0, 1, 0), (1, 0, 0), (0, 0, 1)
     panel_x, panel_y, panel_xy = panel_of(*X), panel_of(*Y), panel_of(1, 1, 0)
 
     def part(k, half):
@@ -186,24 +200,38 @@
         for copy in own_hidden[i]:
             copy.wait()
 
-    def held(half):
-        return pl.ds(half * half_rows, half_rows)
-
-    def quarter(k):
-        return pl.ds(k * part_cols, part_cols)
-
-    own_grad, stage1, own_pick, stage2 = [], [], [], []
-    for half in range(HALVES):
-        for s in range(1, teams):
-            target = (t + s) % teams
-            stage1.append(
-                remote(
-                    grad_ref.at[part(target, half)],
-                    gz.at[held(half), quarter(t)],
-                    (b, target, d),
-                )
+    piece_rows = part_rows // PIECES
+    per_half = PIECES // HALVES
+
+    def landing(shard, panel, q):
+        return gfull.at[
+            shard, pl.ds((q // per_half) * panels + panel, 1), pl.ds(q % per_half * piece_rows, piece_rows)
+        ]
+
+    own_grad, own_pick, stage2 = [], [], []
+    chain_base = send_sem.shape[0] - 2 * (teams - 1) * PIECES
+    stage1_base = chain_base - (teams - 1) * PIECES
+
+    def band(k, q):
+        return pl.ds(k * part_rows + q * piece_rows, piece_rows)
+
+    def spread(up, step, q, action):
+        target = t + step if up else t - step
+
+        @pl.when((target >= 0) & (target < teams))
+        def _():
+            at = stage1_base + (target + teams - t) % teams * PIECES - PIECES + q
+            copy = remote(
+                grad_ref.at[band(target, q)],
+                gz.at[q, :, pl.ds(t * part_cols, part_cols)],
+                (b, target, d),
+                at,
             )
-        own_grad.append(within(grad_ref.at[part(t, half)], gz.at[held(half), quarter(t)]))
+            action(copy)
+
+    def spread_start(step, q):
+        for up in (True, False):
+            spread(up, step, q, lambda copy: copy.start())
 
     def fetch_tables():
         return [within(owner_ref, owner), within(act_ref, act)]
@@ -230,38 +258,38 @@
 
         lax.fori_loop(0, picks, column, 0)
 
-    def pick_columns(half):
-        own_grad[half].wait()
-        for copy in stage1[half * (teams - 1) : (half + 1) * (teams - 1)]:
-            copy.wait_recv()
-        rows = slice(half * half_rows, (half + 1) * half_rows)
+    def pick_columns(q):
+        own_grad[q].wait()
+        for step in range(1, teams):
+            spread(True, step, q, lambda copy: copy.wait_recv())
+            spread(False, step, q, lambda copy: copy.wait_recv())
         for c in range(column_blocks):
-            gcol[half, c] = gz[rows, c * BS : (c + 1) * BS]
-        gcol[half, column_blocks] = jnp.zeros(gcol.shape[2:], gcol.dtype)
+            gcol[q, c] = gz[q, :, c * BS : (c + 1) * BS]
+        gcol[q, column_blocks] = jnp.zeros(gcol.shape[2:], gcol.dtype)
 
         def pick(p, carry):
             for j in range(picks):
-                snd[half, p, :, j * BS : (j + 1) * BS] = gcol[half, cols[0, p * picks + j]]
+                snd[q, p, :, j * BS : (j + 1) * BS] = gcol[q, cols[0, p * picks + j]]
             return carry
 
         lax.fori_loop(0, panels, pick, 0)
-        landing = gfull.at[t, place(mine, half)]
         for flip in flips:
-            stage2.append(remote(snd.at[half, panel_of(*flip)], landing, device(*flip)))
-        own_pick.append(within(snd.at[half, mine], landing))
-
-    def picked(half):
-        own_pick[half].wait()
-        for copy in stage2[half * len(flips) : (half + 1) * len(flips)]:
+            stage2.append(
+                remote(snd.at[q, pl.ds(panel_of(*flip), 1)], landing(t, mine, q), device(*flip))
+            )
+        own_pick.append(within(snd.at[q, pl.ds(mine, 1)], landing(t, mine, q)))
+
+    def picked(q):
+        own_pick[q].wait()
+        for copy in stage2[q * len(flips) : (q + 1) * len(flips)]:
             copy.wait_recv()
 
-    chain_base = send_sem.shape[0] - 2 * (teams - 1) * HALVES
-    chain_rows = panels * half_rows
-
-    def chain(up, k, shard, target, half):
-        piece = gfull.at[shard, pl.ds(half * chain_rows, chain_rows)]
+    def chain(up, k, shard, target, q):
+        piece = gfull.at[
+            shard, pl.ds((q // per_half) * panels, panels), pl.ds(q % per_half * piece_rows, piece_rows)
+        ]
         step = k if up else teams - 1 + k
-        return remote(piece, piece, (b, target, d), chain_base + step * HALVES + half)
+        return remote(piece, piece, (b, target, d), chain_base + step * PIECES + q)
 
     def chain_send(k, half, wait):
         @pl.when((t < teams - 1) & (t - k >= 0))
@@ -288,7 +316,7 @@
 
     def accumulate(i, lo, hi):
         def column(j, carry):
-            g = gfull[shards[i], :, pl.ds(pl.multiple_of(j * BS, BS), BS)]
+            g = gfull[shards[i], :, :, pl.ds(pl.multiple_of(j * BS, BS), BS)].reshape(-1, BS)
             for k in range(0, per_column, GROUP):
                 first = j * per_column + k
                 block = products(slots[i], rows_ref, first, GROUP, g)
@@ -299,43 +327,71 @@
         lax.fori_loop(lo, hi, column, 0)
 
     middle = picks // 2
+    start_own(0)
+    for q in range(PIECES):
+        own_grad.append(
+            within(grad_ref.at[band(t, q)], gz.at[q, :, pl.ds(t * part_cols, part_cols)])
+        )
+    early = PIECES // 2
+    for q in range(early):
+        spread_start(1, q)
     tables = fetch_tables()
-    start_own(0)
+    for k in range(1, max(3, teams - 1)):
+        met(ready.at[k - 1])
+        if k < max(3, teams - 1) - 1:
+            greet(ready.at[k])
+        if k + 1 < teams:
+            for q in range(early):
+                spread_start(k + 1, q)
+    for q in range(early, PIECES):
+        for k in range(1, teams):
+            spread_start(k, q)
     for copy in tables:
         copy.wait()
     own_columns()
     moved = within(cols_row, cols)
     moved.wait()
     pick_columns(0)
+    pick_columns(1)
     turn(0)
-    pick_columns(1)
-    for i in range(teams):
-        if i:
-            turn(i)
+    pick_columns(2)
+    picked(0)
+    chain_send(0, 0, False)
+    pick_columns(3)
+    start_own(1)
+    picked(1)
+    chain_send(0, 1, False)
+    rest(0)
+    picked(2)
+    chain_send(0, 2, False)
+    picked(3)
+    chain_send(0, 3, False)
+    own_rows()
+    corner(0)
+    arrived(0)
+    accumulate(0, 0, middle)
+    for i in range(1, teams):
+        chain_step(i - 1, 0)
+        turn(i)
         if i + 1 < teams:
             start_own(i + 1)
-        if i == 0:
-            picked(0)
-            chain_send(0, 0, False)
-            rest(0)
-            own_rows()
-            corner(0)
-            picked(1)
-            chain_send(0, 1, False)
-        else:
-            chain_step(i - 1, 0)
-            accumulate(i - 1, middle, picks)
-            rest(i)
-            chain_step(i - 1, 1)
-            corner(i)
+        chain_step(i - 1, 1)
+        accumulate(i - 1, middle, picks)
+        chain_step(i - 1, 2)
+        rest(i)
+        corner(i)
+        chain_step(i - 1, 3)
         arrived(i)
         if i + 1 < teams:
             accumulate(i, 0, middle)
     for copy in sent:
         copy.wait_send()
-    for k in range(teams - 1):
-        for half in range(HALVES):
-            chain_send(k, half, True)
+    for q in range(PIECES):
+        for k in range(1, teams):
+            spread(True, k, q, lambda copy: copy.wait_send())
+            spread(False, k, q, lambda copy: copy.wait_send())
+        for k in range(teams - 1):
+            chain_send(k, q, True)
 
 
 def gather(col_owner, act_rows, hidden, out_grad, panels, picks):
@@ -344,10 +400,11 @@
     per_column = act_rows.shape[0]
     part_rows = panel_rows // teams
     half_rows = part_rows // HALVES
+    piece_rows = part_rows // PIECES
     group = panels * part_rows
     column_blocks = col_owner.shape[0]
     lanes = pl.cdiv(panels * picks, BS) * BS
-    copies = (3 * (teams - 1) + panels - 1) * HALVES + 7 * HALVES * teams
+    copies = (3 * (teams - 1) + panels - 1) * PIECES + 7 * HALVES * teams
     operands = (col_owner, act_rows, hidden, out_grad)
     hbm = pl.BlockSpec(memory_space=pltpu.HBM)
     smem = pl.BlockSpec(memory_space=pltpu.SMEM)
@@ -356,7 +413,7 @@
         gather_kernel,
         out_shape=(
             pltpu.VMEM((group, units), hidden.dtype),
-            pltpu.VMEM((teams, group, picks * BS), out_grad.dtype),
+            pltpu.VMEM((teams, HALVES * panels, half_rows, picks * BS), out_grad.dtype),
             pltpu.VMEM((picks * per_column, BS, BS), jnp.float32),
             pltpu.SMEM((picks * per_column,), jnp.int32),
         ),
@@ -364,16 +421,17 @@
         out_specs=(vmem, vmem, vmem, smem),
         scratch_shapes=[pltpu.VMEM((group, units), hidden.dtype)] * (teams - 1)
         + [
-            pltpu.VMEM((part_rows, column_blocks * BS), out_grad.dtype),
-            pltpu.VMEM((HALVES, column_blocks + 1, half_rows, BS), out_grad.dtype),
-            pltpu.VMEM((HALVES, panels, half_rows, picks * BS), out_grad.dtype),
+            pltpu.VMEM((PIECES, piece_rows, column_blocks * BS), out_grad.dtype),
+            pltpu.VMEM((PIECES, column_blocks + 1, piece_rows, BS), out_grad.dtype),
+            pltpu.VMEM((PIECES, panels, piece_rows, picks * BS), out_grad.dtype),
             pltpu.SMEM(col_owner.shape, jnp.int32),
             pltpu.SMEM(act_rows.shape, jnp.int32),
             pltpu.VMEM((1, lanes), jnp.int32),
             pltpu.SMEM((1, lanes), jnp.int32),
+            pltpu.SemaphoreType.REGULAR((max(3, teams - 1) - 1,)),
             pltpu.SemaphoreType.DMA((copies,)),
             pltpu.SemaphoreType.DMA((copies,)),
-            pltpu.SemaphoreType.DMA((HALVES * (2 + teams) + 3,)),
+            pltpu.SemaphoreType.DMA((2 * PIECES + HALVES * teams + 3,)),
         ],
         compiler_params=pltpu.CompilerParams(
             collective_id=0, has_side_effects=True, vmem_limit_bytes=24 << 20
@@ -383,14 +441,14 @@
 
 def finish_kernel(rows_ref, h_ref, g_ref, acc_ref, out_ref, score_ref, buf, ssq, row, sem):
     teams = g_ref.shape[0]
-    picks = g_ref.shape[2] // BS
+    picks = g_ref.shape[-1] // BS
     slots = buf.shape[0]
     per_column = slots // picks
     shard = shard_of(teams - 1, lax.axis_index("team"), teams)
     ssq[slots:] = jnp.zeros((ssq.shape[0] - slots, BS), jnp.float32)
     copies = []
     for j in range(picks):
-        g = g_ref[shard, :, j * BS : (j + 1) * BS]
+        g = g_ref[shard, :, :, j * BS : (j + 1) * BS].reshape(-1, BS)
         for first in range(j * per_column, (j + 1) * per_column, GROUP):
             at = slice(first, first + GROUP)
             block = acc_ref[at] + products(h_ref, rows_ref, first, GROUP, g)
@@ -410,7 +468,7 @@
 
 def finish(rows, last, grad, acc):
     slots = rows.shape[0]
-    picks = grad.shape[2] // BS
+    picks = grad.shape[-1] // BS
     hbm = pl.BlockSpec(memory_space=pltpu.HBM)
     smem = pl.BlockSpec(memory_space=pltpu.SMEM)
     vmem = pl.BlockSpec(memory_space=pltpu.VMEM)

time: 84.6 us -> 81.8 us (0.967)
  Pallas kernels: 83.8 us -> 81 us
    pallas_call x1, Pallas kernels: 79.2 us -> 76.5 us  [gather(): pl.pallas_call(gather_kernel, out_shape=(pltpu.VMEM((group, units), hidde...]
where the time goes in v3:
time: 81.8 us; the launch traced here: 81.7 us
  Pallas kernels  81 us (99%)
    pallas_call x1, Pallas kernels, gather(): pl.pallas_call(gather_kernel, out_shape=(pltpu.VMEM((group, units), hidde...  76.5 us
    pallas_call x1, Pallas kernels, finish(): pl.pallas_call(finish_kernel, out_shape=(jax.ShapeDtypeStruct((slots, BS,...  4.54 us

profile of v3, /device:TPU:0, one launch (start us, length us, event | category | flops | bytes accessed | tf_op | source)
XLA Modules:
  0.0 81.7 jit_solution(14768035573472677437)
XLA Ops:
  0.6 76.5 %shard_map.59 = (bf16[256,7168]{1,0:T(8,128)(2,1)S(1)}, bf16[4,16,16,1536]{3,2,1,0:T(8,128)(2,1)S(1)}, f32[144,128,128]{2,1,0:T(8,128)S(1)}, s32[144]{0:T(256)S(4)}) custom-call(s32[64]{0:T(128)} %owner_ref.1, s32[12,1,64]{2,1,0:T(1,128)} %bitcast.3, bf16[128,7168]{1,0:T(8,128)(2,1)} %hid_ref.1, bf16[128,2048]{1,0:T(8,128)(2,1)} %grad_ref.1), custom_call_target="tpu_custom_call" | custom-call | tf_op jit(solution)/shard_map/pallas_call | solution.py:412
  77.1 4.5 %shard_map.60 = (f32[144,128,128]{2,1,0:T(8,128)}, f32[1,144]{1,0:T(1,128)}) custom-call(s32[144]{0:T(256)S(4)} %get-tuple-element.8.rows_ref, bf16[256,7168]{1,0:T(8,128)(2,1)S(1)} %get-tuple-element.9.h_ref, bf16[4,16,16,1536]{3,2,1,0:T(8,128)(2,1)S(1)} %get-tuple-element.10.g_ref, f32[144,128,128]{2,1,0:T(8,128)S(1)} %get-tuple-element.11.acc_ref), custom_call_target="tpu_custom_call" | custom-call | tf_op jit(solution)/shard_map/pallas_call | solution.py:475

commit v4 on v3

--- a/solution.py
+++ b/solution.py
@@ -9,6 +9,7 @@
 MESH = pl.DeviceIdType.MESH
 HALVES = 2
 PIECES = 4
+TAIL = 4
 GROUP = 4
 
 
@@ -108,7 +109,15 @@
         pl.semaphore_wait(sem, 3 + below + above)
 
     greet(barrier)
-    met(barrier)
+    for step in range(2, teams):
+
+        @pl.when(t + step < teams)
+        def _():
+            pl.semaphore_signal(
+                barrier, inc=1, device_id=(b, t + step, d), device_id_type=MESH
+            )
+
+    pl.semaphore_wait(barrier, 3 + below + above + jnp.maximum(t - 1, 0))
     greet(ready.at[0])
 
     counter = [0, 0]
@@ -138,61 +147,96 @@
         copy.start()
         return copy
 
-    panel_x, panel_y, panel_xy = panel_of(*X), panel_of(*Y), panel_of(1, 1, 0)
+    from_me, by_x, by_y, by_xy = 0, 2, 4, 6
 
     def part(k, half):
         return pl.ds(k * part_rows + half * half_rows, half_rows)
 
-    def place(panel, half):
-        return pl.ds((half * panels + panel) * half_rows, half_rows)
+    def place(rel, half):
+        return pl.ds(rel * part_rows + half * half_rows, half_rows)
 
     shards = [shard_of(i, t, teams) for i in range(teams)]
-
-    def send_own(flip, i, half):
+    units = hid_ref.shape[1]
+
+    def cuts(parts):
+        return [pl.ds(k * (units // parts), units // parts) for k in range(parts)]
+
+    def send_own(flip, i, half, cut=slice(None)):
+        rel = flip[0] * 4 + flip[1] * 2 + flip[2]
         return remote(
-            hid_ref.at[part(shards[i], half)], slots[i].at[place(mine, half)], device(*flip)
+            hid_ref.at[part(shards[i], half), cut],
+            slots[i].at[place(rel, half), cut],
+            device(*flip),
         )
 
-    def forward(panel, flip, i, half):
-        piece = slots[i].at[place(panel, half)]
-        return remote(piece, piece, device(*flip))
+    def forward(rel, flip, i, half, cut=slice(None)):
+        there = rel ^ (flip[0] * 4 + flip[1] * 2 + flip[2])
+        return remote(
+            slots[i].at[place(rel, half), cut],
+            slots[i].at[place(there, half), cut],
+            device(*flip),
+        )
 
     from_x, from_y, from_xy = {}, {}, {}
     from_sib = [[] for _ in range(teams)]
     own_hidden = [[] for _ in range(teams)]
 
-    def start_own(i):
-        from_x[i, 0] = send_own(X, i, 0)
-        from_y[i, 1] = send_own(Y, i, 1)
-        from_x[i, 1] = send_own(X, i, 1)
-        from_y[i, 0] = send_own(Y, i, 0)
+    def start_own(i, cut=None):
+        if cut in (None, 0):
+            from_x[i, 0] = [send_own(X, i, 0)]
+            from_y[i, 1] = [send_own(Y, i, 1)]
+            from_x[i, 1], from_y[i, 0] = [], []
+        pieces = [slice(None)] if cut is None else [cuts(2)[cut]]
+        for piece in pieces:
+            from_x[i, 1].append(send_own(X, i, 1, piece))
+            from_y[i, 0].append(send_own(Y, i, 0, piece))
+        if cut == 0:
+            return
         for half in range(HALVES):
             from_sib[i].append(send_own(SIB, i, half))
             own_hidden[i].append(
-                within(hid_ref.at[part(shards[i], half)], slots[i].at[place(mine, half)])
+                within(hid_ref.at[part(shards[i], half)], slots[i].at[place(from_me, half)])
             )
 
-    def sibling(panel, i, half):
-        from_sib[i].append(forward(panel, SIB, i, half))
+    def received(copies):
+        for copy in copies:
+            copy.wait_recv()
+
+    def sibling(rel, i, half, cut=slice(None)):
+        from_sib[i].append(forward(rel, SIB, i, half, cut))
+
+    both = []
+
+    def bands(i):
+        if i < teams - 1:
+            return [slice(None)]
+        return [pl.ds(0, units - units // TAIL), pl.ds(units - units // TAIL, units // TAIL)]
 
     def turn(i):
-        from_x[i, 0].wait_recv()
-        from_xy[i, 0] = forward(panel_x, Y, i, 0)
-        from_y[i, 1].wait_recv()
-        from_xy[i, 1] = forward(panel_y, X, i, 1)
-        sibling(panel_x, i, 0)
-        sibling(panel_y, i, 1)
+        received(from_x[i, 0])
+        from_xy[i, 0] = [forward(by_x, Y, i, 0, cut) for cut in bands(i)]
+        received(from_y[i, 1])
+        from_xy[i, 1] = [forward(by_y, X, i, 1, cut) for cut in bands(i)]
+        if i == teams - 1:
+            both.append(forward(by_x, (1, 0, 1), i, 0, bands(i)[1]))
+            both.append(forward(by_y, (0, 1, 1), i, 1, bands(i)[1]))
+        sibling(by_x, i, 0)
+        sibling(by_y, i, 1)
 
     def rest(i):
-        from_x[i, 1].wait_recv()
-        sibling(panel_x, i, 1)
-        from_y[i, 0].wait_recv()
-        sibling(panel_y, i, 0)
+        received(from_x[i, 1])
+        sibling(by_x, i, 1)
+        received(from_y[i, 0])
+        sibling(by_y, i, 0)
 
     def corner(i):
         for half in range(HALVES):
-            from_xy[i, half].wait_recv()
-            sibling(panel_xy, i, half)
+            received(from_xy[i, half][:1])
+            sibling(by_xy, i, half, bands(i)[0])
+        for half in range(HALVES):
+            received(from_xy[i, half][1:])
+        if i == teams - 1:
+            received(both)
 
     def arrived(i):
         for copy in from_sib[i]:
@@ -201,12 +245,9 @@
             copy.wait()
 
     piece_rows = part_rows // PIECES
-    per_half = PIECES // HALVES
-
-    def landing(shard, panel, q):
-        return gfull.at[
-            shard, pl.ds((q // per_half) * panels + panel, 1), pl.ds(q % per_half * piece_rows, piece_rows)
-        ]
+
+    def landing(shard, rel, q):
+        return gfull.at[shard, pl.ds(rel, 1), pl.ds(q * piece_rows, piece_rows)]
 
     own_grad, own_pick, stage2 = [], [], []
     chain_base = send_sem.shape[0] - 2 * (teams - 1) * PIECES
@@ -229,9 +270,8 @@
             )
             action(copy)
 
-    def spread_start(step, q):
-        for up in (True, False):
-            spread(up, step, q, lambda copy: copy.start())
+    def spread_start(up, step, q):
+        spread(up, step, q, lambda copy: copy.start())
 
     def fetch_tables():
         return [within(owner_ref, owner), within(act_ref, act)]
@@ -275,9 +315,13 @@
         lax.fori_loop(0, panels, pick, 0)
         for flip in flips:
             stage2.append(
-                remote(snd.at[q, pl.ds(panel_of(*flip), 1)], landing(t, mine, q), device(*flip))
+                remote(
+                    snd.at[q, pl.ds(panel_of(*flip), 1)],
+                    landing(t, flip[0] * 4 + flip[1] * 2 + flip[2], q),
+                    device(*flip),
+                )
             )
-        own_pick.append(within(snd.at[q, pl.ds(mine, 1)], landing(t, mine, q)))
+        own_pick.append(within(snd.at[q, pl.ds(mine, 1)], landing(t, from_me, q)))
 
     def picked(q):
         own_pick[q].wait()
@@ -285,9 +329,7 @@
             copy.wait_recv()
 
     def chain(up, k, shard, target, q):
-        piece = gfull.at[
-            shard, pl.ds((q // per_half) * panels, panels), pl.ds(q % per_half * piece_rows, piece_rows)
-        ]
+        piece = gfull.at[shard, pl.ds(0, panels), pl.ds(q * piece_rows, piece_rows)]
         step = k if up else teams - 1 + k
         return remote(piece, piece, (b, target, d), chain_base + step * PIECES + q)
 
@@ -327,14 +369,16 @@
         lax.fori_loop(lo, hi, column, 0)
 
     middle = picks // 2
-    start_own(0)
+    start_own(0, 0)
     for q in range(PIECES):
         own_grad.append(
             within(grad_ref.at[band(t, q)], gz.at[q, :, pl.ds(t * part_cols, part_cols)])
         )
     early = PIECES // 2
     for q in range(early):
-        spread_start(1, q)
+        for k in range(teams - 1, 0, -1):
+            spread_start(False, k, q)
+        spread_start(True, 1, q)
     tables = fetch_tables()
     for k in range(1, max(3, teams - 1)):
         met(ready.at[k - 1])
@@ -342,28 +386,30 @@
             greet(ready.at[k])
         if k + 1 < teams:
             for q in range(early):
-                spread_start(k + 1, q)
+                spread_start(True, k + 1, q)
     for q in range(early, PIECES):
-        for k in range(1, teams):
-            spread_start(k, q)
+        for k in range(teams - 1, 0, -1):
+            spread_start(False, k, q)
+            spread_start(True, k, q)
     for copy in tables:
         copy.wait()
     own_columns()
     moved = within(cols_row, cols)
     moved.wait()
     pick_columns(0)
+    start_own(0, 1)
     pick_columns(1)
-    turn(0)
     pick_columns(2)
     picked(0)
     chain_send(0, 0, False)
     pick_columns(3)
+    turn(0)
     start_own(1)
     picked(1)
     chain_send(0, 1, False)
-    rest(0)
     picked(2)
     chain_send(0, 2, False)
+    rest(0)
     picked(3)
     chain_send(0, 3, False)
     own_rows()
@@ -399,12 +445,11 @@
     panel_rows, units = hidden.shape
     per_column = act_rows.shape[0]
     part_rows = panel_rows // teams
-    half_rows = part_rows // HALVES
     piece_rows = part_rows // PIECES
     group = panels * part_rows
     column_blocks = col_owner.shape[0]
     lanes = pl.cdiv(panels * picks, BS) * BS
-    copies = (3 * (teams - 1) + panels - 1) * PIECES + 7 * HALVES * teams
+    copies = (3 * (teams - 1) + panels - 1) * PIECES + 7 * HALVES * teams + 6
     operands = (col_owner, act_rows, hidden, out_grad)
     hbm = pl.BlockSpec(memory_space=pltpu.HBM)
     smem = pl.BlockSpec(memory_space=pltpu.SMEM)
@@ -413,7 +458,7 @@
         gather_kernel,
         out_shape=(
             pltpu.VMEM((group, units), hidden.dtype),
-            pltpu.VMEM((teams, HALVES * panels, half_rows, picks * BS), out_grad.dtype),
+            pltpu.VMEM((teams, panels, part_rows, picks * BS), out_grad.dtype),
             pltpu.VMEM((picks * per_column, BS, BS), jnp.float32),
             pltpu.SMEM((picks * per_column,), jnp.int32),
         ),

time: 81.8 us -> 81.5 us (level)
  no operation moved by 1% of the time
where the time goes in v4:
time: 81.5 us; the launch traced here: 81.4 us
  Pallas kernels  80.8 us (99%)
    pallas_call x1, Pallas kernels, gather(): pl.pallas_call(gather_kernel, out_shape=(pltpu.VMEM((group, units), hidde...  76.2 us
    pallas_call x1, Pallas kernels, finish(): pl.pallas_call(finish_kernel, out_shape=(jax.ShapeDtypeStruct((slots, BS,...  4.53 us

profile of v4, /device:TPU:0, one launch (start us, length us, event | category | flops | bytes accessed | tf_op | source)
XLA Modules:
  0.0 81.4 jit_solution(14458724911659338360)
XLA Ops:
  0.6 76.2 %shard_map.59 = (bf16[256,7168]{1,0:T(8,128)(2,1)S(1)}, bf16[4,8,32,1536]{3,2,1,0:T(8,128)(2,1)S(1)}, f32[144,128,128]{2,1,0:T(8,128)S(1)}, s32[144]{0:T(256)S(4)}) custom-call(s32[64]{0:T(128)} %owner_ref.1, s32[12,1,64]{2,1,0:T(1,128)} %bitcast.3, bf16[128,7168]{1,0:T(8,128)(2,1)} %hid_ref.1, bf16[128,2048]{1,0:T(8,128)(2,1)} %grad_ref.1), custom_call_target="tpu_custom_call" | custom-call | tf_op jit(solution)/shard_map/pallas_call | solution.py:457
  76.9 4.5 %shard_map.60 = (f32[144,128,128]{2,1,0:T(8,128)}, f32[1,144]{1,0:T(1,128)}) custom-call(s32[144]{0:T(256)S(4)} %get-tuple-element.8.rows_ref, bf16[256,7168]{1,0:T(8,128)(2,1)S(1)} %get-tuple-element.9.h_ref, bf16[4,8,32,1536]{3,2,1,0:T(8,128)(2,1)S(1)} %get-tuple-element.10.g_ref, f32[144,128,128]{2,1,0:T(8,128)S(1)} %get-tuple-element.11.acc_ref), custom_call_target="tpu_custom_call" | custom-call | tf_op jit(solution)/shard_map/pallas_call | solution.py:520

commit v5 on v4

--- a/solution.py
+++ b/solution.py
@@ -11,6 +11,7 @@
 PIECES = 4
 TAIL = 4
 GROUP = 4
+LAST = 3
 
 
 epsilon = 1e-06
@@ -368,14 +369,24 @@
 
         lax.fori_loop(lo, hi, column, 0)
 
+    def settle():
+        for copy in sent[:early]:
+            copy.wait_send()
+        for q in range(PIECES):
+            for k in range(1, teams):
+                spread(True, k, q, lambda copy: copy.wait_send())
+                spread(False, k, q, lambda copy: copy.wait_send())
+            for k in range(teams - 2):
+                chain_send(k, q, True)
+
     middle = picks // 2
     start_own(0, 0)
     for q in range(PIECES):
         own_grad.append(
             within(grad_ref.at[band(t, q)], gz.at[q, :, pl.ds(t * part_cols, part_cols)])
         )
-    early = PIECES // 2
-    for q in range(early):
+    first = PIECES // 2
+    for q in range(first):
         for k in range(teams - 1, 0, -1):
             spread_start(False, k, q)
         spread_start(True, 1, q)
@@ -385,9 +396,9 @@
         if k < max(3, teams - 1) - 1:
             greet(ready.at[k])
         if k + 1 < teams:
-            for q in range(early):
+            for q in range(first):
                 spread_start(True, k + 1, q)
-    for q in range(early, PIECES):
+    for q in range(first, PIECES):
         for k in range(teams - 1, 0, -1):
             spread_start(False, k, q)
             spread_start(True, k, q)
@@ -418,6 +429,7 @@
     accumulate(0, 0, middle)
     for i in range(1, teams):
         chain_step(i - 1, 0)
+        early = len(sent)
         turn(i)
         if i + 1 < teams:
             start_own(i + 1)
@@ -425,19 +437,17 @@
         accumulate(i - 1, middle, picks)
         chain_step(i - 1, 2)
         rest(i)
+        if i + 1 == teams:
+            settle()
         corner(i)
         chain_step(i - 1, 3)
         arrived(i)
         if i + 1 < teams:
             accumulate(i, 0, middle)
-    for copy in sent:
+    for copy in sent[early:]:
         copy.wait_send()
     for q in range(PIECES):
-        for k in range(1, teams):
-            spread(True, k, q, lambda copy: copy.wait_send())
-            spread(False, k, q, lambda copy: copy.wait_send())
-        for k in range(teams - 1):
-            chain_send(k, q, True)
+        chain_send(teams - 2, q, True)
 
 
 def gather(col_owner, act_rows, hidden, out_grad, panels, picks):
@@ -494,9 +504,9 @@
     copies = []
     for j in range(picks):
         g = g_ref[shard, :, :, j * BS : (j + 1) * BS].reshape(-1, BS)
-        for first in range(j * per_column, (j + 1) * per_column, GROUP):
-            at = slice(first, first + GROUP)
-            block = acc_ref[at] + products(h_ref, rows_ref, first, GROUP, g)
+        for first in range(j * per_column, (j + 1) * per_column, LAST):
+            at = slice(first, first + LAST)
+            block = acc_ref[at] + products(h_ref, rows_ref, first, LAST, g)
             buf[at] = block
             ssq[at, :] = jnp.sum(block * block, axis=1)
         done = pl.ds(j * per_column, per_column)

time: 81.5 us -> 81.3 us (level)
  no operation moved by 1% of the time
where the time goes in v5:
time: 81.3 us; the launch traced here: 81.1 us
  Pallas kernels  80.5 us (99%)
    pallas_call x1, Pallas kernels, gather(): pl.pallas_call(gather_kernel, out_shape=(pltpu.VMEM((group, units), hidde...  76.2 us
    pallas_call x1, Pallas kernels, finish(): pl.pallas_call(finish_kernel, out_shape=(jax.ShapeDtypeStruct((slots, BS,...  4.32 us

profile of v5, /device:TPU:0, one launch (start us, length us, event | category | flops | bytes accessed | tf_op | source)
XLA Modules:
  0.0 81.1 jit_solution(10339851987500189930)
XLA Ops:
  0.6 76.2 %shard_map.59 = (bf16[256,7168]{1,0:T(8,128)(2,1)S(1)}, bf16[4,8,32,1536]{3,2,1,0:T(8,128)(2,1)S(1)}, f32[144,128,128]{2,1,0:T(8,128)S(1)}, s32[144]{0:T(256)S(4)}) custom-call(s32[64]{0:T(128)} %owner_ref.1, s32[12,1,64]{2,1,0:T(1,128)} %bitcast.3, bf16[128,7168]{1,0:T(8,128)(2,1)} %hid_ref.1, bf16[128,2048]{1,0:T(8,128)(2,1)} %grad_ref.1), custom_call_target="tpu_custom_call" | custom-call | tf_op jit(solution)/shard_map/pallas_call | solution.py:467
  76.8 4.3 %shard_map.60 = (f32[144,128,128]{2,1,0:T(8,128)}, f32[1,144]{1,0:T(1,128)}) custom-call(s32[144]{0:T(256)S(4)} %get-tuple-element.8.rows_ref, bf16[256,7168]{1,0:T(8,128)(2,1)S(1)} %get-tuple-element.9.h_ref, bf16[4,8,32,1536]{3,2,1,0:T(8,128)(2,1)S(1)} %get-tuple-element.10.g_ref, f32[144,128,128]{2,1,0:T(8,128)S(1)} %get-tuple-element.11.acc_ref), custom_call_target="tpu_custom_call" | custom-call | tf_op jit(solution)/shard_map/pallas_call | solution.py:530

commit v6 on v5

--- a/solution.py
+++ b/solution.py
@@ -306,7 +306,6 @@
             spread(False, step, q, lambda copy: copy.wait_recv())
         for c in range(column_blocks):
             gcol[q, c] = gz[q, :, c * BS : (c + 1) * BS]
-        gcol[q, column_blocks] = jnp.zeros(gcol.shape[2:], gcol.dtype)
 
         def pick(p, carry):
             for j in range(picks):
@@ -405,6 +404,8 @@
     for copy in tables:
         copy.wait()
     own_columns()
+    for q in range(PIECES):
+        gcol[q, column_blocks] = jnp.zeros(gcol.shape[2:], gcol.dtype)
     moved = within(cols_row, cols)
     moved.wait()
     pick_columns(0)

time: 81.3 us -> 81.3 us (level)
  no operation moved by 1% of the time
where the time goes in v6:
time: 81.3 us; the launch traced here: 81.2 us
  Pallas kernels  80.5 us (99%)
    pallas_call x1, Pallas kernels, gather(): pl.pallas_call(gather_kernel, out_shape=(pltpu.VMEM((group, units), hidde...  76.2 us
    pallas_call x1, Pallas kernels, finish(): pl.pallas_call(finish_kernel, out_shape=(jax.ShapeDtypeStruct((slots, BS,...  4.33 us

profile of v6, /device:TPU:0, one launch (start us, length us, event | category | flops | bytes accessed | tf_op | source)
XLA Modules:
  0.0 81.2 jit_solution(15513722161496406942)
XLA Ops:
  0.6 76.2 %shard_map.59 = (bf16[256,7168]{1,0:T(8,128)(2,1)S(1)}, bf16[4,8,32,1536]{3,2,1,0:T(8,128)(2,1)S(1)}, f32[144,128,128]{2,1,0:T(8,128)S(1)}, s32[144]{0:T(256)S(4)}) custom-call(s32[64]{0:T(128)} %owner_ref.1, s32[12,1,64]{2,1,0:T(1,128)} %bitcast.3, bf16[128,7168]{1,0:T(8,128)(2,1)} %hid_ref.1, bf16[128,2048]{1,0:T(8,128)(2,1)} %grad_ref.1), custom_call_target="tpu_custom_call" | custom-call | tf_op jit(solution)/shard_map/pallas_call | solution.py:468
  76.8 4.3 %shard_map.60 = (f32[144,128,128]{2,1,0:T(8,128)}, f32[1,144]{1,0:T(1,128)}) custom-call(s32[144]{0:T(256)S(4)} %get-tuple-element.8.rows_ref, bf16[256,7168]{1,0:T(8,128)(2,1)S(1)} %get-tuple-element.9.h_ref, bf16[4,8,32,1536]{3,2,1,0:T(8,128)(2,1)S(1)} %get-tuple-element.10.g_ref, f32[144,128,128]{2,1,0:T(8,128)S(1)} %get-tuple-element.11.acc_ref), custom_call_target="tpu_custom_call" | custom-call | tf_op jit(solution)/shard_map/pallas_call | solution.py:531

commit v7 on v6

--- a/solution.py
+++ b/solution.py
@@ -510,14 +510,16 @@
             block = acc_ref[at] + products(h_ref, rows_ref, first, LAST, g)
             buf[at] = block
             ssq[at, :] = jnp.sum(block * block, axis=1)
-        done = pl.ds(j * per_column, per_column)
-        copies.append(pltpu.make_async_copy(buf.at[done], out_ref.at[done], sem.at[j]))
-        copies[j].start()
+            if (first + LAST) % (per_column // 2) == 0:
+                done = pl.ds(first + LAST - per_column // 2, per_column // 2)
+                at_sem = sem.at[len(copies)]
+                copies.append(pltpu.make_async_copy(buf.at[done], out_ref.at[done], at_sem))
+                copies[-1].start()
     total = jnp.sum(ssq[...].T, axis=0, keepdims=True)
     scores = jnp.sqrt(total * (1.0 / (BS * BS)) + epsilon)
     row[...] = scores[:, :slots]
-    copies.append(pltpu.make_async_copy(row, score_ref, sem.at[picks]))
-    copies[picks].start()
+    copies.append(pltpu.make_async_copy(row, score_ref, sem.at[2 * picks]))
+    copies[-1].start()
     for copy in copies:
         copy.wait()
 
@@ -540,7 +542,7 @@
             pltpu.VMEM((slots, BS, BS), jnp.float32),
             pltpu.VMEM((pl.cdiv(slots, BS) * BS, BS), jnp.float32),
             pltpu.VMEM((1, slots), jnp.float32),
-            pltpu.SemaphoreType.DMA((picks + 1,)),
+            pltpu.SemaphoreType.DMA((2 * picks + 1,)),
         ],
         compiler_params=pltpu.CompilerParams(vmem_limit_bytes=20 << 20),
     )(rows, last, grad, acc)

time: 81.3 us -> 81.3 us (level)
  no operation moved by 1% of the time
where the time goes in v7:
time: 81.3 us; the launch traced here: 81.1 us
  Pallas kernels  80.5 us (99%)
    pallas_call x1, Pallas kernels, gather(): pl.pallas_call(gather_kernel, out_shape=(pltpu.VMEM((group, units), hidde...  76.2 us
    pallas_call x1, Pallas kernels, finish(): pl.pallas_call(finish_kernel, out_shape=(jax.ShapeDtypeStruct((slots, BS,...  4.29 us

profile of v7, /device:TPU:0, one launch (start us, length us, event | category | flops | bytes accessed | tf_op | source)
XLA Modules:
  0.0 81.1 jit_solution(2503450107489869134)
XLA Ops:
  0.6 76.2 %shard_map.59 = (bf16[256,7168]{1,0:T(8,128)(2,1)S(1)}, bf16[4,8,32,1536]{3,2,1,0:T(8,128)(2,1)S(1)}, f32[144,128,128]{2,1,0:T(8,128)S(1)}, s32[144]{0:T(256)S(4)}) custom-call(s32[64]{0:T(128)} %owner_ref.1, s32[12,1,64]{2,1,0:T(1,128)} %bitcast.3, bf16[128,7168]{1,0:T(8,128)(2,1)} %hid_ref.1, bf16[128,2048]{1,0:T(8,128)(2,1)} %grad_ref.1), custom_call_target="tpu_custom_call" | custom-call | tf_op jit(solution)/shard_map/pallas_call | solution.py:468
  76.8 4.3 %shard_map.60 = (f32[144,128,128]{2,1,0:T(8,128)}, f32[1,144]{1,0:T(1,128)}) custom-call(s32[144]{0:T(256)S(4)} %get-tuple-element.8.rows_ref, bf16[256,7168]{1,0:T(8,128)(2,1)S(1)} %get-tuple-element.9.h_ref, bf16[4,8,32,1536]{3,2,1,0:T(8,128)(2,1)S(1)} %get-tuple-element.10.g_ref, f32[144,128,128]{2,1,0:T(8,128)S(1)} %get-tuple-element.11.acc_ref), custom_call_target="tpu_custom_call" | custom-call | tf_op jit(solution)/shard_map/pallas_call | solution.py:533
